TPU v7x, 32 devices: a whole 2x2x4 slice. The times are simulated.
32 devices in a mesh: shard: 2 (over x), ctx: 4 (over y, core), tp: 4 (over z).
Axes of the slice: x: 2, y: 2, z: 4, core: 2. Of those that a mesh axis runs over, the one named last changes fastest.
Arguments:
- tokens: bfloat16 [8, 1024, 767], P('shard', 'ctx'), may hold values from -6 to 6
- lengths: int32 [8], P('shard'), may hold values from 256 to 1024, as said below
- first_gain: float32 [768], replicated, may hold values from 0.5 to 1.5
- entry_weight: bfloat16 [3, 768, 768], P(None, ('shard', 'ctx'), 'tp'), may hold values from -0.21875 to 0.21875
- entry_bias: float32 [2, 768], P(None, 'tp'), may hold values from -3 to 3
- exit_weight: bfloat16 [768, 768], P('tp', ('shard', 'ctx')), may hold values from -0.625 to 0.625
- exit_bias: float32 [768], replicated, may hold values from -3 to 3
- second_gain: float32 [768], replicated, may hold values from 0.5 to 1.5
- hidden_weight: bfloat16 [768, 3072], P(('shard', 'ctx'), 'tp'), may hold values from -0.21875 to 0.21875
- hidden_bias: float32 [3072], P('tp'), may hold values from -3 to 3
- return_weight: bfloat16 [3072, 768], P('tp', ('shard', 'ctx')), may hold values from -0.109375 to 0.109375
- return_bias: float32 [768], replicated, may hold values from -3 to 3
- cotangent: bfloat16 [8, 1024, 767], P('shard', 'ctx'), may hold values from -6 to 6
Outputs:
- result: bfloat16 [8, 1024, 767], P('shard', 'ctx')
- tokens_gradient: bfloat16 [8, 1024, 767], P('shard', 'ctx')
- first_gain_gradient: float32 [768], replicated
- entry_weight_gradient: float32 [3, 768, 768], P(None, ('shard', 'ctx'), 'tp')
- entry_bias_gradient: float32 [2, 768], P(None, 'tp')
- exit_weight_gradient: float32 [768, 768], P('tp', ('shard', 'ctx'))
- exit_bias_gradient: float32 [768], replicated
- second_gain_gradient: float32 [768], replicated
- hidden_weight_gradient: float32 [768, 3072], P(('shard', 'ctx'), 'tp')
- hidden_bias_gradient: float32 [3072], P('tp')
- return_weight_gradient: float32 [3072, 768], P('tp', ('shard', 'ctx'))
- return_bias_gradient: float32 [768], replicated
Inputs may be any that keep to these rules, and one draw needn't show every extreme that they name: `lengths`: in every draw some sequence has exactly 1024 valid positions and some has exactly 256.
All inputs are finite; a program needn't handle non-finite values.
Results may differ from a plain program's by a relative error of at most 0.014.
Values may be sent and summed in bfloat16 or wider, within the bound.
No kernel may reach another device: no remote copies, remote signals or barrier semaphores. Data moves between devices by JAX's collectives and lax.ppermute only.
A program may use at most 256 MiB of HBM per device.

v0:
```python
import math
import jax
import jax.numpy as jnp
from jax import lax
from jax.sharding import PartitionSpec as P

HDIM = 64
EPSILON = 1e-05


def row_mean(values):
    return jnp.mean(values, -1, keepdims=True)


def shards(
    tokens,
    lengths,
    first_gain,
    entry_weight,
    entry_bias,
    exit_weight,
    exit_bias,
    second_gain,
    hidden_weight,
    hidden_bias,
    return_weight,
    return_bias,
    cotangent,
):
    seq_dev, local, narrow = tokens.shape
    row_count = seq_dev * local
    full_len = local * lax.axis_size("ctx")
    head_width = entry_weight.shape[2]
    heads_here = head_width // HDIM
    scale = 1.0 / math.sqrt(HDIM)
    bfloat = jnp.bfloat16
    single = jnp.float32
    full_entry, full_exit, full_hidden, full_return = (
        lax.all_gather(entry_weight, ("shard", "ctx"), axis=1, tiled=True),
        lax.all_gather(exit_weight, ("shard", "ctx"), axis=1, tiled=True),
        lax.all_gather(hidden_weight, ("shard", "ctx"), axis=0, tiled=True),
        lax.all_gather(return_weight, ("shard", "ctx"), axis=1, tiled=True),
    )
    stream_part = tokens.astype(single).reshape(row_count, narrow)
    stream = jnp.concatenate([stream_part, -jnp.sum(stream_part, -1, keepdims=True)], 1)
    first_inverse = lax.rsqrt(row_mean(stream * stream) + EPSILON)
    first_unit = stream * first_inverse
    first_normed = (first_unit * first_gain).astype(bfloat)
    queries = (
        jnp.dot(first_normed, full_entry[0], preferred_element_type=single) + entry_bias[0]
    ).astype(bfloat)
    keys = jnp.dot(first_normed, full_entry[1], preferred_element_type=single).astype(bfloat)
    values = (
        jnp.dot(first_normed, full_entry[2], preferred_element_type=single) + entry_bias[1]
    ).astype(bfloat)
    seq_shape = (seq_dev, local, head_width)
    all_keys, all_values = (
        lax.all_gather(keys.reshape(seq_shape), "ctx", axis=1, tiled=True),
        lax.all_gather(values.reshape(seq_shape), "ctx", axis=1, tiled=True),
    )
    offset = lax.axis_index("ctx") * local
    query_pos = offset + jnp.arange(local, dtype=jnp.int32)
    key_pos = jnp.arange(full_len, dtype=jnp.int32)
    local_heads = (seq_dev, local, heads_here, HDIM)
    full_heads = (seq_dev, full_len, heads_here, HDIM)
    allowed = (
        (key_pos[None, None, :] <= query_pos[None, :, None])
        & (key_pos[None, None, :] < lengths[:, None, None])
    )[:, None]

    def masked_scores(query_block, key_block):
        raw_scores = (
            jnp.einsum("sqhd,skhd->shqk", query_block, key_block, preferred_element_type=single)
            * scale
        )
        return jnp.where(allowed, raw_scores, -1e30)

    query_heads = queries.reshape(local_heads)
    scores = masked_scores(query_heads, all_keys.reshape(full_heads))
    largest = jnp.max(scores, -1, keepdims=True)
    exponent = jnp.exp(scores - largest)
    totals = jnp.sum(exponent, -1, keepdims=True)
    weights = (exponent / totals).astype(bfloat)
    log_totals = largest + jnp.log(totals)
    attended = jnp.einsum(
        "shqk,skhd->sqhd", weights, all_values.reshape(full_heads), preferred_element_type=single
    ).astype(bfloat)
    attended_rows = attended.reshape(row_count, head_width)
    exit_term = jnp.dot(attended_rows, full_exit, preferred_element_type=single)
    branch = lax.psum(exit_term, "tp") + exit_bias
    middle = stream + branch - row_mean(branch)
    second_inverse = lax.rsqrt(row_mean(middle * middle) + EPSILON)
    second_unit = middle * second_inverse
    second_normed = (second_unit * second_gain).astype(bfloat)
    hidden = jnp.dot(second_normed, full_hidden, preferred_element_type=single) + hidden_bias
    activated, gelu_pull = jax.vjp(
        lambda values_in: jax.nn.gelu(values_in, approximate=True), hidden
    )
    activated_low = activated.astype(bfloat)
    return_term = jnp.dot(activated_low, full_return, preferred_element_type=single)
    returned = lax.psum(return_term.astype(jnp.bfloat16), "tp").astype(jnp.float32) + return_bias
    full_stream = middle + returned - row_mean(returned)
    result_rows = full_stream[:, :narrow].astype(bfloat)
    result = result_rows.reshape(seq_dev, local, narrow)
    full_entry, full_exit, full_hidden, full_return = (
        lax.all_gather(entry_weight, ("shard", "ctx"), axis=1, tiled=True),
        lax.all_gather(exit_weight, ("shard", "ctx"), axis=1, tiled=True),
        lax.all_gather(hidden_weight, ("shard", "ctx"), axis=0, tiled=True),
        lax.all_gather(return_weight, ("shard", "ctx"), axis=1, tiled=True),
    )
    valid = (query_pos[None, :] < lengths[:, None]).astype(single).reshape(row_count, 1)
    cot_rows = cotangent.astype(single).reshape(row_count, narrow) * valid
    cot_full = jnp.concatenate([cot_rows, jnp.zeros((row_count, 1), single)], 1)
    returned_grad = (cot_full - row_mean(cot_full)).astype(bfloat)
    return_bias_grad = jnp.sum(returned_grad.astype(single), 0)
    return_weight_grad = jnp.einsum(
        "rf,rd->fd", activated_low, returned_grad, preferred_element_type=single
    )
    activated_grad = jnp.einsum(
        "rd,fd->rf", returned_grad, full_return, preferred_element_type=single
    )
    hidden_grad = gelu_pull(activated_grad)[0].astype(bfloat)
    hidden_bias_grad = jnp.sum(hidden_grad.astype(single), 0)
    hidden_weight_grad = jnp.einsum(
        "rd,rf->df", second_normed, hidden_grad, preferred_element_type=single
    )
    second_term = jnp.einsum("rf,df->rd", hidden_grad, full_hidden, preferred_element_type=single)
    second_grad = lax.psum(second_term, "tp")
    second_gain_grad = jnp.sum(second_grad * second_unit, 0)
    second_scaled = second_grad * second_gain
    middle_grad = cot_full + second_inverse * (
        second_scaled - second_unit * row_mean(second_scaled * second_unit)
    )
    branch_grad = (middle_grad - row_mean(middle_grad)).astype(bfloat)
    exit_bias_grad = jnp.sum(branch_grad.astype(single), 0)
    exit_weight_grad = jnp.einsum(
        "re,rd->ed", attended_rows, branch_grad, preferred_element_type=single
    )
    attended_grad = jnp.einsum(
        "rd,ed->re", branch_grad, full_exit, preferred_element_type=single
    ).astype(bfloat)
    all_keys, all_values = (
        lax.all_gather(keys.reshape(seq_shape), "ctx", axis=1, tiled=True),
        lax.all_gather(values.reshape(seq_shape), "ctx", axis=1, tiled=True),
    )
    key_heads = all_keys.reshape(full_heads)
    value_heads = all_values.reshape(full_heads)
    out_grad = attended_grad.reshape(local_heads)
    back_scores = masked_scores(query_heads, key_heads)
    probs = jnp.exp(back_scores - log_totals)
    probs_low = probs.astype(bfloat)
    prob_rounded = lax.optimization_barrier(
        jnp.einsum("sqhd,skhd->shqk", out_grad, value_heads, preferred_element_type=single).astype(
            bfloat
        )
    )
    prob_grad = prob_rounded.astype(single)
    inner = jnp.sum(probs * prob_grad, -1, keepdims=True)
    score_grad = (probs * (prob_grad - inner)).astype(bfloat)
    query_grads = (
        jnp.einsum("shqk,skhd->sqhd", score_grad, key_heads, preferred_element_type=single) * scale
    ).astype(bfloat)
    key_parts = (
        jnp.einsum("shqk,sqhd->skhd", score_grad, query_heads, preferred_element_type=single)
        * scale
    )
    value_parts = jnp.einsum("shqk,sqhd->skhd", probs_low, out_grad, preferred_element_type=single)
    key_sums, value_sums = (
        lax.psum_scatter(
            key_parts.reshape(seq_dev, full_len, head_width), "ctx", scatter_dimension=1, tiled=True
        ),
        lax.psum_scatter(
            value_parts.reshape(seq_dev, full_len, head_width),
            "ctx",
            scatter_dimension=1,
            tiled=True,
        ),
    )
    query_low = query_grads.reshape(row_count, head_width)
    key_low = key_sums.reshape(row_count, head_width).astype(bfloat)
    value_low = value_sums.reshape(row_count, head_width).astype(bfloat)
    entry_bias_grad = jnp.stack(
        [jnp.sum(query_low.astype(single), 0), jnp.sum(value_low.astype(single), 0)]
    )
    entry_weight_grad = jnp.stack(
        [
            jnp.einsum("rd,re->de", first_normed, query_low, preferred_element_type=single),
            jnp.einsum("rd,re->de", first_normed, key_low, preferred_element_type=single),
            jnp.einsum("rd,re->de", first_normed, value_low, preferred_element_type=single),
        ]
    )
    first_part = (
        jnp.einsum("re,de->rd", query_low, full_entry[0], preferred_element_type=single)
        + jnp.einsum("re,de->rd", key_low, full_entry[1], preferred_element_type=single)
        + jnp.einsum("re,de->rd", value_low, full_entry[2], preferred_element_type=single)
    )
    first_grad = lax.psum(first_part, "tp")
    first_gain_grad = jnp.sum(first_grad * first_unit, 0)
    first_scaled = first_grad * first_gain
    stream_grad = middle_grad + first_inverse * (
        first_scaled - first_unit * row_mean(first_scaled * first_unit)
    )
    tokens_rows = (stream_grad[:, :narrow] - stream_grad[:, narrow:]).astype(bfloat)
    tokens_grad = tokens_rows.reshape(seq_dev, local, narrow)
    weight_grads = (
        lax.psum_scatter(entry_weight_grad, ("shard", "ctx"), scatter_dimension=1, tiled=True),
        lax.psum_scatter(exit_weight_grad, ("shard", "ctx"), scatter_dimension=1, tiled=True),
        lax.psum_scatter(hidden_weight_grad, ("shard", "ctx"), scatter_dimension=0, tiled=True),
        lax.psum_scatter(return_weight_grad, ("shard", "ctx"), scatter_dimension=1, tiled=True),
    )
    small_grads = lax.psum(
        (
            first_gain_grad,
            entry_bias_grad,
            exit_bias_grad,
            second_gain_grad,
            hidden_bias_grad,
            return_bias_grad,
        ),
        ("shard", "ctx"),
    )
    return (
        result,
        tokens_grad,
        small_grads[0],
        weight_grads[0],
        small_grads[1],
        weight_grads[1],
        small_grads[2],
        small_grads[3],
        weight_grads[2],
        small_grads[4],
        weight_grads[3],
        small_grads[5],
    )


def solution(mesh):
    return jax.shard_map(
        shards,
        mesh=mesh,
        in_specs=(
            P("shard", "ctx", None),
            P("shard"),
            P(),
            P(None, ("shard", "ctx"), "tp"),
            P(None, "tp"),
            P("tp", ("shard", "ctx")),
            P(),
            P(),
            P(("shard", "ctx"), "tp"),
            P("tp"),
            P("tp", ("shard", "ctx")),
            P(),
            P("shard", "ctx", None),
        ),
        out_specs=(
            P("shard", "ctx", None),
            P("shard", "ctx", None),
            P(),
            P(None, ("shard", "ctx"), "tp"),
            P(None, "tp"),
            P("tp", ("shard", "ctx")),
            P(),
            P(),
            P(("shard", "ctx"), "tp"),
            P("tp"),
            P("tp", ("shard", "ctx")),
            P(),
        ),
        check_vma=False,
    )
```

profile of v0, /device:TPU:0, one launch (start us, length us, event | category | flops | bytes accessed | tf_op | source)
XLA Modules:
  0.0 1059.9 jit_solution(7665863335763462059)
XLA Ops:
  8.1 2.3 convert_reduce_fusion.5
  10.3 2.9 copy.52
  14.5 13.1 %all_gather.24 = bf16[3,768,192]{2,1,0:T(8,128)(2,1)S(1)} all-gather(bf16[3,96,192]{2,1,0:T(8,128)(2,1)S(1)} %copy-done.38), channel_id=1, replica_groups=mesh['shard'=2,'ctx'=4,'tp'=4] {'shard','ctx'}, dimensions={1}, use_global_device_ids=true | all-gather | bytes 995328 | tf_op jit(solution)/shard_map/all_gather | solution.py:39
  36.3 2.9 fusion.21
  42.1 12.4 %all_gather.27 = bf16[192,768]{0,1:T(8,128)(2,1)} all-gather(bf16[192,96]{0,1:T(8,128)(2,1)} %copy.58), channel_id=1, replica_groups=mesh['shard'=2,'ctx'=4,'tp'=4] {'shard','ctx'}, dimensions={1}, use_global_device_ids=true | all-gather | bytes 331776 | tf_op jit(solution)/shard_map/all_gather | solution.py:40
  58.6 2.9 fusion.38
  61.6 4.6 copy-done
  66.2 3.4 fusion.3
  69.6 6.6 all-gather.5.cloned.1.call-done
  78.1 6.6 fusion.24
  85.8 2.2 fusion.39
  89.6 4.3 copy.59
  94.0 2.2 bitcast_multiply_fusion
  99.9 109.4 %all-reduce.7.cloned.1.call-done = f32[1024,768]{1,0:T(8,128)} async-done(((f32[1024,768]{1,0:T(8,128)}), f32[1024,768]{1,0:T(8,128)}) %all-reduce.7.cloned.1.call-update) | async-done | bytes 3145744 | tf_op jit(solution)/shard_map/psum | solution.py:90
  209.3 2.2 add_reduce_fusion
  211.6 4.3 multiply_reduce_fusion.4
  215.9 5.5 fusion.33
  221.4 5.6 convert_reduce_fusion.1
  228.2 3.1 fusion.40
  232.5 119.0 %all-reduce.11.cloned.1.call-done = f32[1024,768]{1,0:T(8,128)} async-done(((f32[1024,768]{1,0:T(8,128)}), f32[1024,768]{1,0:T(8,128)}) %all-reduce.11.cloned.1.call-update) | async-done | bytes 3145744 | tf_op jit(solution)/shard_map/psum | solution.py:128
  351.5 3.5 multiply_reduce_fusion
  363.4 7.6 fusion
  371.1 3.0 fusion.2
  376.7 48.2 %copy.69 = f32[4,1024,192]{0,2,1:T(8,128)} copy(f32[4,1024,192]{1,2,0:T(8,128)S(1)} %bitcast.133) | data formatting | bytes 6291456
  424.9 84.3 %reshape.241 = f32[1024,768]{1,0:T(8,128)} reshape(f32[1024,192,4]{2,1,0:T(8,128)} %bitcast.22) | data formatting | bytes 6291456
  509.8 6.3 fusion.5
  516.1 48.3 %copy.71 = f32[4,1024,192]{0,2,1:T(8,128)} copy(f32[4,1024,192]{1,2,0:T(8,128)S(1)} %bitcast.127) | data formatting | bytes 6291456
  564.3 84.3 %reshape.243 = f32[1024,768]{1,0:T(8,128)} reshape(f32[1024,192,4]{2,1,0:T(8,128)} %bitcast.25) | data formatting | bytes 6291456
  649.9 5.1 convolution_convert_fusion.1
  657.0 5.1 convert_reduce_fusion.4
  663.8 29.2 %reshape.242 = bf16[256,192,4]{2,1,0:T(8,128)(2,1)} reshape(f32[256,768]{1,0:T(8,128)} %reduce-scatter.19.cloned.1.call-done) | data formatting | bytes 1179648
  693.0 12.2 %copy.70 = bf16[4,256,192]{1,0,2:T(4,128)(2,1)S(1)} copy(bf16[4,256,192]{0,2,1:T(8,128)(2,1)} %bitcast.123) | data formatting | bytes 786432
  705.3 29.3 %reshape.244 = bf16[256,192,4]{2,1,0:T(8,128)(2,1)} reshape(f32[256,768]{1,0:T(8,128)} %reduce-scatter.21.cloned.1.call-done) | data formatting | bytes 1179648
  734.6 12.2 %copy.72 = bf16[4,256,192]{1,0,2:T(4,128)(2,1)S(1)} copy(bf16[4,256,192]{0,2,1:T(8,128)(2,1)} %bitcast.124) | data formatting | bytes 786432
  749.3 2.9 copy.73
  752.2 2.9 reshape.245
  757.9 2.3 add_add_fusion
  760.4 5.8 fusion.34
  766.3 4.4 fusion.32
  774.1 3.9 copy.66
  778.1 15.8 %reduce-scatter.25.cloned.1.call-done = f32[96,192]{1,0:T(8,128)} async-done(((f32[768,192]{1,0:T(8,128)}), f32[96,192]{1,0:T(8,128)}) %reduce-scatter.25.cloned.1.call-update) | async-done | bytes 73744
  796.5 40.9 %reduce-scatter.23.cloned.1.call-done = f32[96,576]{1,0:T(8,128)} async-done(((f32[768,576]{1,0:T(8,128)}), f32[96,576]{1,0:T(8,128)}) %reduce-scatter.23.cloned.1.call-update) | async-done | bytes 221200
  839.3 121.4 %all-reduce.13.cloned.1.call-done = f32[1024,768]{1,0:T(8,128)} async-done(((f32[1024,768]{1,0:T(8,128)}), f32[1024,768]{1,0:T(8,128)}) %all-reduce.13.cloned.1.call-update) | async-done | bytes 3145744 | tf_op jit(solution)/shard_map/psum | solution.py:197
  960.8 3.0 multiply_reduce_fusion.1
  967.0 2.2 copy.67
  969.2 25.0 %all-reduce.1 = (f32[768]{0:T(1024)}, f32[2,192]{1,0:T(2,128)}, f32[768]{0:T(1024)}, f32[768]{0:T(1024)}, f32[768]{0:T(1024)}, /*index=5*/f32[768]{0:T(1024)}) all-reduce(f32[768]{0:T(1024)S(1)} %get-tuple-element.48, f32[2,192]{1,0:T(2,128)S(1)} %pad_maximum_fusion.2, ...), channel_id=1, replica_groups=mesh['shard'=2,'ctx'=4,'tp'=4] {'shard','ctx'}, use_global_device_ids=true, to_apply=%region_19.20 | all-reduce | flops 4224 | bytes 33792 | tf_op jit(solution)/shard_map/psum | solution.py:211
  994.2 11.9 %reduce-scatter.17.cloned.1.call-done = f32[768,96]{0,1:T(8,128)} async-done(((f32[768,768]{0,1:T(8,128)}), f32[768,96]{0,1:T(8,128)}) %reduce-scatter.17.cloned.1.call-update) | async-done | bytes 294928 | tf_op jit(solution)/shard_map/reduce_scatter | solution.py:209
  1006.1 46.2 %reduce-scatter.15.cloned.1.call-done = f32[96,768]{1,0:T(8,128)} async-done(((f32[768,768]{1,0:T(8,128)}), f32[96,768]{1,0:T(8,128)}) %reduce-scatter.15.cloned.1.call-update) | async-done | bytes 294928 | tf_op jit(solution)/shard_map/reduce_scatter | solution.py:208
  (233 shorter events, 60.3 us)
Async XLA Ops:
  8.0 6.5 copy-start.38
  8.0 48.6 %all-gather.7.cloned.1.call-start = ((), (), s32[]{:S(2)}) async-start(), calls=%async_computation.7 | async-start | bytes 1966080 | tf_op jit(solution)/shard_map/all_gather | solution.py:58
  13.3 198.3 %copy-start.1 = (f32[4,256,767]{2,1,0:T(8,128)}, f32[4,256,767]{2,1,0:T(8,128)S(1)}, u32[]{:S(2)}) copy-start(f32[4,256,767]{2,1,0:T(8,128)S(1)} %copy.52) | copy-start | bytes 9424900
  13.3 16.2 %copy-start.45 = (f32[768]{0:T(1024)S(1)}, f32[768]{0:T(1024)}, u32[]{:S(2)}) copy-start(f32[768]{0:T(1024)} %param.15) | copy-start | bytes 9220
  14.5 15.0 %copy-start.14 = (f32[1,1024]{0,1:T(8,128)S(1)}, f32[1,1024]{0,1:T(8,128)}, u32[]{:S(2)}) copy-start(f32[1,1024]{0,1:T(8,128)} %copy.81) | copy-start | bytes 12292
  33.0 43.2 %all-gather.5.cloned.1.call-start = ((), (), s32[]{:S(2)}) async-start(), calls=%async_computation.6 | async-start | bytes 1966080 | tf_op jit(solution)/shard_map/all_gather | solution.py:59
  33.1 21.4 %copy-start.59 = (s32[4]{0:T(128)S(1)}, s32[4]{0:T(128)}, u32[]{:S(2)}) copy-start(s32[4]{0:T(128)} %param.14) | copy-start | bytes 52
  36.3 173.0 %all-reduce.7.cloned.1.call-start = ((), (), s32[]{:S(2)}) async-start(), calls=%async_computation.8 | async-start | bytes 6291456 | tf_op jit(solution)/shard_map/psum | solution.py:90
  42.0 19.5 %copy-start.26 = (bf16[4,256,3,64]{1,0,3,2:T(4,128)(2,1)}, bf16[4,256,3,64]{1,0,3,2:T(4,128)(2,1)S(1)}, u32[]{:S(2)}) copy-start(bf16[4,256,3,64]{1,0,3,2:T(4,128)(2,1)S(1)} %reshape.226) | copy-start | bytes 1179652
  61.5 4.7 copy-start
  61.5 16.6 %copy-start.37 = (f32[4,3,256]{2,1,0:T(4,128)}, f32[4,3,256]{2,1,0:T(4,128)S(1)}, u32[]{:S(2)}) copy-start(f32[4,3,256]{2,1,0:T(4,128)S(1)} %get-tuple-element.72) | copy-start | bytes 36868
  78.1 6.6 copy-start.23
  78.1 7.7 copy-start.30
  88.1 127.8 %all-gather.9.cloned.1.call-start = ((), (), s32[]{:S(2)}) async-start(), calls=%async_computation.9 | async-start | bytes 1327104 | tf_op jit(solution)/shard_map/all_gather | solution.py:41
  88.7 132.7 %all-gather.11.cloned.1.call-start = ((), (), s32[]{:S(2)}) async-start(), calls=%async_computation.10 | async-start | bytes 1327104 | tf_op jit(solution)/shard_map/all_gather | solution.py:42
  89.3 262.2 %all-reduce.11.cloned.1.call-start = ((), (), s32[]{:S(2)}) async-start(), calls=%async_computation.12 | async-start | bytes 6291456 | tf_op jit(solution)/shard_map/psum | solution.py:128
  96.4 112.9 %copy-start.47 = (f32[768]{0:T(1024)S(1)}, f32[768]{0:T(1024)}, u32[]{:S(2)}) copy-start(f32[768]{0:T(1024)} %param.19) | copy-start | bytes 9220
  211.6 4.3 copy-start.48
  215.9 5.5 copy-start.42
  215.9 5.5 copy-start.36
  215.9 5.5 copy-start.63
  221.4 6.8 copy-start.62
  231.2 120.2 %copy-start.6 = (f32[1024,768]{1,0:T(8,128)S(1)}, f32[1024,768]{1,0:T(8,128)}, u32[]{:S(2)}) copy-start(f32[1024,768]{1,0:T(8,128)} %get-tuple-element.67) | copy-start | bytes 9437188
  231.3 432.5 %reduce-scatter.19.cloned.1.call-start = ((), (), s32[]{:S(2)}) async-start(), calls=%async_computation.16 | async-start | bytes 3932160
  351.5 3.8 copy-start.43
  361.6 9.5 slice-start
  361.6 9.5 slice-start.1
  363.4 7.6 slice-start.2
  509.3 196.1 %reduce-scatter.21.cloned.1.call-start = ((), (), s32[]{:S(2)}) async-start(), calls=%async_computation.17 | async-start | bytes 3932160
  648.7 6.4 copy-start.18
  648.7 6.4 copy-start.35
  648.7 122.0 %all-reduce.9.cloned.1.call-start = ((), (), s32[]{:S(2)}) async-start(), calls=%async_computation.11 | async-start | bytes 3145728 | tf_op jit(solution)/shard_map/psum | solution.py:101
  655.1 138.8 %reduce-scatter.25.cloned.1.call-start = ((), (), s32[]{:S(2)}) async-start(), calls=%async_computation.19 | async-start | bytes 884736
  656.8 6.5 copy-start.5
  656.8 180.6 %reduce-scatter.23.cloned.1.call-start = ((), (), s32[]{:S(2)}) async-start(), calls=%async_computation.18 | async-start | bytes 2211840
  705.3 41.6 %copy-start.32 = (bf16[24,8,4,256]{3,1,2,0:T(8,128)(2,1)}, bf16[24,8,4,256]{3,1,2,0:T(8,128)(2,1)S(1)}, u32[]{:S(2)}) copy-start(bf16[24,8,4,256]{3,1,2,0:T(8,128)(2,1)S(1)} %copy.85) | copy-start | bytes 1179652
  755.1 205.6 %all-reduce.13.cloned.1.call-start = ((), (), s32[]{:S(2)}) async-start(), calls=%async_computation.13 | async-start | bytes 6291456 | tf_op jit(solution)/shard_map/psum | solution.py:197
  760.3 6.0 copy-start.7
  760.3 6.0 copy-start.44
  760.3 6.0 copy-start.50
  760.3 245.8 %reduce-scatter.17.cloned.1.call-start = ((), (), s32[]{:S(2)}) async-start(), calls=%async_computation.15 | async-start | bytes 2654208 | tf_op jit(solution)/shard_map/reduce_scatter | solution.py:209
  766.2 4.6 copy-start.54
  766.2 286.1 %reduce-scatter.15.cloned.1.call-start = ((), (), s32[]{:S(2)}) async-start(), calls=%async_computation.14 | async-start | bytes 2654208 | tf_op jit(solution)/shard_map/reduce_scatter | solution.py:208
  772.6 22.9 %copy-start.29 = (bf16[4,256,192]{1,0,2:T(4,128)(2,1)S(1)}, bf16[4,256,192]{1,0,2:T(4,128)(2,1)}, u32[]{:S(2)}) copy-start(bf16[4,256,192]{1,0,2:T(4,128)(2,1)} %copy-done.28) | copy-start | bytes 1179652
  774.1 186.7 %copy-start.2 = (f32[4,256,767]{2,1,0:T(8,128)S(1)}, f32[4,256,767]{2,1,0:T(8,128)}, u32[]{:S(2)}) copy-start(f32[4,256,767]{2,1,0:T(8,128)} %copy-done.1) | copy-start | bytes 9424900
  774.1 186.7 %copy-start.41 = (f32[1024]{0:T(1024)S(1)}, f32[1024]{0:T(1024)}, u32[]{:S(2)}) copy-start(f32[1024]{0:T(1024)} %copy-done.40) | copy-start | bytes 12292
  774.1 186.7 %copy-start.46 = (f32[768]{0:T(1024)S(1)}, f32[768]{0:T(1024)}, u32[]{:S(2)}) copy-start(f32[768]{0:T(1024)} %param.15) | copy-start | bytes 9220
  960.8 4.1 copy-start.20
  (35 other events, 77.7 us)
Sparse Core Ops, SparseCore 0:
  33.1 21.6 all-gather.6
  56.4 19.7 all-gather.4
  88.2 121.0 all-reduce.6
  231.4 120.0 all-reduce.10
  509.4 36.8 reduce-scatter.18
  648.8 36.3 reduce-scatter.20
  687.6 68.9 all-reduce.8
  759.7 34.0 reduce-scatter.24
  797.3 40.1 reduce-scatter.22
  839.7 121.0 all-reduce.12
  964.7 41.4 reduce-scatter.16
  1009.9 42.3 reduce-scatter.14
Sparse Core Ops, SparseCore 1:
  90.5 23.8 all-gather.8
  116.1 23.8 all-gather.10
where the time goes:
time: 1070 us; the launch traced here: 1060 us
  waiting for transfers between devices  472 us (44%)
  local copies, waits for them, and re-layouts  400 us (37%)
  matrix products  69.9 us (7%)
  blocking collectives  50.5 us (5%)
  other arithmetic  48.4 us (5%)
  between operations  16.9 us (2%)
    unnamed x161, local copies, waits for them, and re-layouts  384 us
    psum x1, waiting for transfers between devices, shards(): first_grad = lax.psum(first_part, 'tp')  121 us
    psum x1, waiting for transfers between devices, shards(): second_grad = lax.psum(second_term, 'tp')  119 us
    psum x1, waiting for transfers between devices, shards(): branch = lax.psum(exit_term, 'tp') + exit_bias  109 us
    unnamed x18, waiting for transfers between devices  58 us
    reduce_scatter x1, waiting for transfers between devices, shards(): lax.psum_scatter(hidden_weight_grad, ('shard', 'ctx'), scatter_dimension=...  46.2 us
    psum x1, blocking collectives, shards(): lax.psum((first_gain_grad, entry_bias_grad, exit_bias_grad, second_gain_g...  25 us
  transfers between devices with their start and end apart: 14, of which 8 were waited for; matrix products, arithmetic and copies ran while one was open for 30% of the time, Pallas kernels for 0%

commit v1 on v0

--- a/solution.py
+++ b/solution.py
@@ -125,7 +125,11 @@
         "rd,rf->df", second_normed, hidden_grad, preferred_element_type=single
     )
     second_term = jnp.einsum("rf,df->rd", hidden_grad, full_hidden, preferred_element_type=single)
-    second_grad = lax.psum(second_term, "tp")
+    second_grad = second_term
+    for hop in (1, 2):
+        second_grad = second_grad + lax.ppermute(
+            second_grad, "tp", [(dev, dev ^ hop) for dev in range(4)]
+        )
     second_gain_grad = jnp.sum(second_grad * second_unit, 0)
     second_scaled = second_grad * second_gain
     middle_grad = cot_full + second_inverse * (

time: 1070 us -> 1150 us (1.075)
  waiting for transfers between devices: 472 us -> 560 us
    ppermute x0 -> x2, waiting for transfers between devices: none -> 205 us  [shards(): lax.ppermute(second_grad, 'tp', [(dev, dev ^ hop) for dev in range(4)])]
    psum x1 -> x0, waiting for transfers between devices: 119 us -> none  [shards(): second_grad = lax.psum(second_term, 'tp')]
    unnamed x18 -> x17, waiting for transfers between devices: 58 us -> 58.8 us
  transfers between devices with their start and end apart: 14 -> 15, of which waited for: 8 -> 9; matrix products, arithmetic and copies ran while one was open for 30% -> 28% of each run, Pallas kernels for 0% -> 0%
where the time goes in v1:
time: 1150 us; the launch traced here: 1140 us
  waiting for transfers between devices  560 us (49%)
  local copies, waits for them, and re-layouts  398 us (35%)
  matrix products  67.9 us (6%)
  blocking collectives  50.5 us (4%)
  other arithmetic  46.9 us (4%)
  between operations  16.6 us (1%)
    unnamed x161, local copies, waits for them, and re-layouts  382 us
    ppermute x2, waiting for transfers between devices, shards(): lax.ppermute(second_grad, 'tp', [(dev, dev ^ hop) for dev in range(4)])  205 us
    psum x1, waiting for transfers between devices, shards(): first_grad = lax.psum(first_part, 'tp')  122 us
    psum x1, waiting for transfers between devices, shards(): branch = lax.psum(exit_term, 'tp') + exit_bias  109 us
    unnamed x17, waiting for transfers between devices  58.8 us
    reduce_scatter x1, waiting for transfers between devices, shards(): lax.psum_scatter(hidden_weight_grad, ('shard', 'ctx'), scatter_dimension=...  46.3 us
    psum x1, blocking collectives, shards(): lax.psum((first_gain_grad, entry_bias_grad, exit_bias_grad, second_gain_g...  25 us
  transfers between devices with their start and end apart: 15, of which 9 were waited for; matrix products, arithmetic and copies ran while one was open for 28% of the time, Pallas kernels for 0%

profile of v1, /device:TPU:0, one launch (start us, length us, event | category | flops | bytes accessed | tf_op | source)
XLA Modules:
  0.0 1142.6 jit_solution(313880302754473780)
XLA Ops:
  8.1 2.3 convert_reduce_fusion.5
  10.3 2.9 copy.52
  14.5 13.1 %all_gather.24 = bf16[3,768,192]{2,1,0:T(8,128)(2,1)S(1)} all-gather(bf16[3,96,192]{2,1,0:T(8,128)(2,1)S(1)} %copy-done.38), channel_id=1, replica_groups=mesh['shard'=2,'ctx'=4,'tp'=4] {'shard','ctx'}, dimensions={1}, use_global_device_ids=true | all-gather | bytes 995328 | tf_op jit(solution)/shard_map/all_gather | solution.py:39
  33.1 2.2 fusion.20
  36.4 2.9 fusion.21
  42.1 12.3 %all_gather.27 = bf16[192,768]{0,1:T(8,128)(2,1)} all-gather(bf16[192,96]{0,1:T(8,128)(2,1)} %copy.58), channel_id=1, replica_groups=mesh['shard'=2,'ctx'=4,'tp'=4] {'shard','ctx'}, dimensions={1}, use_global_device_ids=true | all-gather | bytes 331776 | tf_op jit(solution)/shard_map/all_gather | solution.py:40
  58.6 2.9 fusion.38
  61.5 4.6 copy-done
  66.2 3.4 fusion.3
  69.5 6.7 all-gather.5.cloned.1.call-done
  78.1 6.6 fusion.24
  85.8 2.2 fusion.39
  89.6 4.3 copy.59
  93.9 2.2 bitcast_multiply_fusion
  99.8 109.5 %all-reduce.6.cloned.1.call-done = f32[1024,768]{1,0:T(8,128)} async-done(((f32[1024,768]{1,0:T(8,128)}), f32[1024,768]{1,0:T(8,128)}) %all-reduce.6.cloned.1.call-update) | async-done | bytes 3145744 | tf_op jit(solution)/shard_map/psum | solution.py:90
  209.3 2.2 add_reduce_fusion
  211.6 4.3 multiply_reduce_fusion.4
  215.9 5.5 fusion.33
  221.4 5.6 convert_reduce_fusion.1
  228.6 69.7 %collective-permute-done = f32[1024,768]{1,0:T(8,128)S(1)} collective-permute-done((f32[1024,768]{1,0:T(8,128)S(1)}, f32[1024,768]{1,0:T(8,128)S(1)}, u32[]{:S(2)}, u32[]{:S(2)}) %collective-permute-start) | collective-permute-done | bytes 3145760 | tf_op jit(solution)/shard_map/ppermute | solution.py:130
  300.4 135.7 %collective-permute-done.1 = f32[1024,768]{1,0:T(8,128)S(1)} collective-permute-done((f32[1024,768]{1,0:T(8,128)S(1)}, f32[1024,768]{1,0:T(8,128)S(1)}, u32[]{:S(2)}, u32[]{:S(2)}) %collective-permute-start.1) | collective-permute-done | bytes 3145760 | tf_op jit(solution)/shard_map/ppermute | solution.py:130
  446.2 7.8 fusion
  454.1 3.0 fusion.2
  459.6 48.1 %copy.69 = f32[4,1024,192]{0,2,1:T(8,128)} copy(f32[4,1024,192]{1,2,0:T(8,128)S(1)} %bitcast.133) | data formatting | bytes 6291456
  507.8 84.3 %reshape.241 = f32[1024,768]{1,0:T(8,128)} reshape(f32[1024,192,4]{2,1,0:T(8,128)} %bitcast.22) | data formatting | bytes 6291456
  592.2 5.8 fusion.5
  598.0 48.1 %copy.71 = f32[4,1024,192]{0,2,1:T(8,128)} copy(f32[4,1024,192]{1,2,0:T(8,128)S(1)} %bitcast.127) | data formatting | bytes 6291456
  646.1 84.4 %reshape.243 = f32[1024,768]{1,0:T(8,128)} reshape(f32[1024,192,4]{2,1,0:T(8,128)} %bitcast.25) | data formatting | bytes 6291456
  731.8 5.1 convolution_convert_fusion.1
  738.7 5.3 convert_reduce_fusion.4
  745.6 29.2 %reshape.242 = bf16[256,192,4]{2,1,0:T(8,128)(2,1)} reshape(f32[256,768]{1,0:T(8,128)} %reduce-scatter.19.cloned.1.call-done) | data formatting | bytes 1179648
  774.8 12.4 %copy.70 = bf16[4,256,192]{1,0,2:T(4,128)(2,1)S(1)} copy(bf16[4,256,192]{0,2,1:T(8,128)(2,1)} %bitcast.123) | data formatting | bytes 786432
  787.3 29.3 %reshape.244 = bf16[256,192,4]{2,1,0:T(8,128)(2,1)} reshape(f32[256,768]{1,0:T(8,128)} %reduce-scatter.21.cloned.1.call-done) | data formatting | bytes 1179648
  816.6 12.2 %copy.72 = bf16[4,256,192]{1,0,2:T(4,128)(2,1)S(1)} copy(bf16[4,256,192]{0,2,1:T(8,128)(2,1)} %bitcast.124) | data formatting | bytes 786432
  831.2 3.0 copy.73
  834.2 2.9 reshape.245
  839.9 2.3 add_add_fusion
  842.3 5.8 fusion.34
  848.2 4.4 fusion.32
  856.0 3.9 copy.66
  860.0 16.6 %reduce-scatter.25.cloned.1.call-done = f32[96,192]{1,0:T(8,128)} async-done(((f32[768,192]{1,0:T(8,128)}), f32[96,192]{1,0:T(8,128)}) %reduce-scatter.25.cloned.1.call-update) | async-done | bytes 73744
  879.3 40.9 %reduce-scatter.23.cloned.1.call-done = f32[96,576]{1,0:T(8,128)} async-done(((f32[768,576]{1,0:T(8,128)}), f32[96,576]{1,0:T(8,128)}) %reduce-scatter.23.cloned.1.call-update) | async-done | bytes 221200
  922.1 121.6 %all-reduce.10.cloned.1.call-done = f32[1024,768]{1,0:T(8,128)} async-done(((f32[1024,768]{1,0:T(8,128)}), f32[1024,768]{1,0:T(8,128)}) %all-reduce.10.cloned.1.call-update) | async-done | bytes 3145744 | tf_op jit(solution)/shard_map/psum | solution.py:201
  1043.7 3.0 multiply_reduce_fusion.1
  1049.9 2.2 copy.67
  1052.2 25.0 %all-reduce.1 = (f32[768]{0:T(1024)}, f32[2,192]{1,0:T(2,128)}, f32[768]{0:T(1024)}, f32[768]{0:T(1024)}, f32[768]{0:T(1024)}, /*index=5*/f32[768]{0:T(1024)}) all-reduce(f32[768]{0:T(1024)S(1)} %get-tuple-element.50, f32[2,192]{1,0:T(2,128)S(1)} %pad_maximum_fusion.2, ...), channel_id=1, replica_groups=mesh['shard'=2,'ctx'=4,'tp'=4] {'shard','ctx'}, use_global_device_ids=true, to_apply=%region_18.19 | all-reduce | flops 4224 | bytes 33792 | tf_op jit(solution)/shard_map/psum | solution.py:215
  1077.1 11.7 %reduce-scatter.17.cloned.1.call-done = f32[768,96]{0,1:T(8,128)} async-done(((f32[768,768]{0,1:T(8,128)}), f32[768,96]{0,1:T(8,128)}) %reduce-scatter.17.cloned.1.call-update) | async-done | bytes 294928 | tf_op jit(solution)/shard_map/reduce_scatter | solution.py:213
  1088.9 46.3 %reduce-scatter.15.cloned.1.call-done = f32[96,768]{1,0:T(8,128)} async-done(((f32[768,768]{1,0:T(8,128)}), f32[96,768]{1,0:T(8,128)}) %reduce-scatter.15.cloned.1.call-update) | async-done | bytes 294928 | tf_op jit(solution)/shard_map/reduce_scatter | solution.py:212
  (235 shorter events, 60.3 us)
Async XLA Ops:
  8.0 6.5 copy-start.38
  8.0 48.6 %all-gather.7.cloned.1.call-start = ((), (), s32[]{:S(2)}) async-start(), calls=%async_computation.7 | async-start | bytes 1966080 | tf_op jit(solution)/shard_map/all_gather | solution.py:58
  13.3 198.3 %copy-start.1 = (f32[4,256,767]{2,1,0:T(8,128)}, f32[4,256,767]{2,1,0:T(8,128)S(1)}, u32[]{:S(2)}) copy-start(f32[4,256,767]{2,1,0:T(8,128)S(1)} %copy.52) | copy-start | bytes 9424900
  13.3 16.2 %copy-start.45 = (f32[768]{0:T(1024)S(1)}, f32[768]{0:T(1024)}, u32[]{:S(2)}) copy-start(f32[768]{0:T(1024)} %param.15) | copy-start | bytes 9220
  14.5 15.0 %copy-start.14 = (f32[1,1024]{0,1:T(8,128)S(1)}, f32[1,1024]{0,1:T(8,128)}, u32[]{:S(2)}) copy-start(f32[1,1024]{0,1:T(8,128)} %copy.81) | copy-start | bytes 12292
  33.0 43.2 %all-gather.5.cloned.1.call-start = ((), (), s32[]{:S(2)}) async-start(), calls=%async_computation.6 | async-start | bytes 1966080 | tf_op jit(solution)/shard_map/all_gather | solution.py:59
  33.1 21.4 %copy-start.59 = (s32[4]{0:T(128)S(1)}, s32[4]{0:T(128)}, u32[]{:S(2)}) copy-start(s32[4]{0:T(128)} %param.14) | copy-start | bytes 52
  36.3 173.0 %all-reduce.6.cloned.1.call-start = ((), (), s32[]{:S(2)}) async-start(), calls=%async_computation.8 | async-start | bytes 6291456 | tf_op jit(solution)/shard_map/psum | solution.py:90
  42.1 19.4 %copy-start.25 = (bf16[4,256,3,64]{1,0,3,2:T(4,128)(2,1)}, bf16[4,256,3,64]{1,0,3,2:T(4,128)(2,1)S(1)}, u32[]{:S(2)}) copy-start(bf16[4,256,3,64]{1,0,3,2:T(4,128)(2,1)S(1)} %reshape.226) | copy-start | bytes 1179652
  61.5 16.6 %copy-start.36 = (f32[4,3,256]{2,1,0:T(4,128)}, f32[4,3,256]{2,1,0:T(4,128)S(1)}, u32[]{:S(2)}) copy-start(f32[4,3,256]{2,1,0:T(4,128)S(1)} %get-tuple-element.72) | copy-start | bytes 36868
  78.1 6.6 copy-start.22
  78.1 7.7 copy-start.29
  88.1 127.8 %all-gather.9.cloned.1.call-start = ((), (), s32[]{:S(2)}) async-start(), calls=%async_computation.9 | async-start | bytes 1327104 | tf_op jit(solution)/shard_map/all_gather | solution.py:41
  88.7 132.7 %all-gather.11.cloned.1.call-start = ((), (), s32[]{:S(2)}) async-start(), calls=%async_computation.10 | async-start | bytes 1327104 | tf_op jit(solution)/shard_map/all_gather | solution.py:42
  89.3 656.3 %reduce-scatter.19.cloned.1.call-start = ((), (), s32[]{:S(2)}) async-start(), calls=%async_computation.15 | async-start | bytes 3932160
  96.4 113.0 %copy-start.47 = (f32[768]{0:T(1024)S(1)}, f32[768]{0:T(1024)}, u32[]{:S(2)}) copy-start(f32[768]{0:T(1024)} %param.19) | copy-start | bytes 9220
  215.9 221.8 %copy-start.43 = (f32[1024]{0:T(1024)}, f32[1024]{0:T(1024)S(1)}, u32[]{:S(2)}) copy-start(f32[1024]{0:T(1024)S(1)} %add_rsqrt_fusion) | copy-start | bytes 12292
  215.9 5.5 copy-start.35
  215.9 5.5 copy-start.63
  221.4 5.6 copy-start.62
  228.4 71.9 %copy-start.37 = (f32[4,3,256]{2,1,0:T(4,128)S(1)}, f32[4,3,256]{2,1,0:T(4,128)}, u32[]{:S(2)}) copy-start(f32[4,3,256]{2,1,0:T(4,128)} %copy-done.36) | copy-start | bytes 36868
  228.5 71.9 %copy-start.40 = (f32[4,3,256]{2,1,0:T(4,128)S(1)}, f32[4,3,256]{2,1,0:T(4,128)}, u32[]{:S(2)}) copy-start(f32[4,3,256]{2,1,0:T(4,128)} %fusion.3) | copy-start | bytes 36868
  228.5 207.6 %copy-start.6 = (f32[1024,768]{1,0:T(8,128)S(1)}, f32[1024,768]{1,0:T(8,128)}, u32[]{:S(2)}) copy-start(f32[1024,768]{1,0:T(8,128)} %get-tuple-element.67) | copy-start | bytes 9437188
  228.5 207.6 %copy-start.49 = (f32[768]{0:T(1024)S(1)}, f32[768]{0:T(1024)}, u32[]{:S(2)}) copy-start(f32[768]{0:T(1024)} %param.20) | copy-start | bytes 9220
  228.5 69.7 %collective-permute-start = (f32[1024,768]{1,0:T(8,128)S(1)}, f32[1024,768]{1,0:T(8,128)S(1)}, u32[]{:S(2)}, u32[]{:S(2)}) collective-permute-start(f32[1024,768]{1,0:T(8,128)S(1)} %fusion.40), channel_id=1, source_target_pairs={{0,1},{1,0},{2,3},{3,2},{4,5},{5,4},{6,7},{7,6},{8,9},{9,8},{10,11... | collective-permute-start | bytes 9437192 | tf_op jit(solution)/shard_map/ppermute | solution.py:130
  298.9 137.2 %collective-permute-start.1 = (f32[1024,768]{1,0:T(8,128)S(1)}, f32[1024,768]{1,0:T(8,128)S(1)}, u32[]{:S(2)}, u32[]{:S(2)}) collective-permute-start(f32[1024,768]{1,0:T(8,128)S(1)} %add.165), channel_id=1, source_target_pairs={{0,2},{1,3},{2,0},{3,1},{4,6},{5,7},{6,4},{7,5},{8,10},{9,11},{10,... | collective-permute-start | bytes 9437192 | tf_op jit(solution)/shard_map/ppermute | solution.py:130
  300.4 137.3 %copy-start.9 = (f32[1024,767]{1,0:T(8,128)S(1)}, f32[1024,767]{1,0:T(8,128)}, u32[]{:S(2)}) copy-start(f32[1024,767]{1,0:T(8,128)} %copy-done.8) | copy-start | bytes 9424900
  444.3 9.7 slice-start
  444.3 9.7 slice-start.1
  446.1 7.9 slice-start.2
  592.1 195.2 %reduce-scatter.21.cloned.1.call-start = ((), (), s32[]{:S(2)}) async-start(), calls=%async_computation.16 | async-start | bytes 3932160
  730.5 6.5 copy-start.18
  730.5 6.5 copy-start.34
  730.5 122.2 %all-reduce.8.cloned.1.call-start = ((), (), s32[]{:S(2)}) async-start(), calls=%async_computation.11 | async-start | bytes 3145728 | tf_op jit(solution)/shard_map/psum | solution.py:101
  736.9 139.7 %reduce-scatter.25.cloned.1.call-start = ((), (), s32[]{:S(2)}) async-start(), calls=%async_computation.18 | async-start | bytes 884736
  738.6 6.5 copy-start.5
  738.6 181.6 %reduce-scatter.23.cloned.1.call-start = ((), (), s32[]{:S(2)}) async-start(), calls=%async_computation.17 | async-start | bytes 2211840
  787.3 41.6 %copy-start.31 = (bf16[24,8,4,256]{3,1,2,0:T(8,128)(2,1)}, bf16[24,8,4,256]{3,1,2,0:T(8,128)(2,1)S(1)}, u32[]{:S(2)}) copy-start(bf16[24,8,4,256]{3,1,2,0:T(8,128)(2,1)S(1)} %copy.85) | copy-start | bytes 1179652
  837.1 206.6 %all-reduce.10.cloned.1.call-start = ((), (), s32[]{:S(2)}) async-start(), calls=%async_computation.12 | async-start | bytes 6291456 | tf_op jit(solution)/shard_map/psum | solution.py:201
  842.3 6.0 copy-start.7
  842.3 6.0 copy-start.44
  842.3 6.0 copy-start.50
  842.3 246.6 %reduce-scatter.17.cloned.1.call-start = ((), (), s32[]{:S(2)}) async-start(), calls=%async_computation.14 | async-start | bytes 2654208 | tf_op jit(solution)/shard_map/reduce_scatter | solution.py:213
  848.2 287.0 %reduce-scatter.15.cloned.1.call-start = ((), (), s32[]{:S(2)}) async-start(), calls=%async_computation.13 | async-start | bytes 2654208 | tf_op jit(solution)/shard_map/reduce_scatter | solution.py:212
  854.5 23.7 %copy-start.28 = (bf16[4,256,192]{1,0,2:T(4,128)(2,1)S(1)}, bf16[4,256,192]{1,0,2:T(4,128)(2,1)}, u32[]{:S(2)}) copy-start(bf16[4,256,192]{1,0,2:T(4,128)(2,1)} %copy-done.27) | copy-start | bytes 1179652
  856.0 187.6 %copy-start.2 = (f32[4,256,767]{2,1,0:T(8,128)S(1)}, f32[4,256,767]{2,1,0:T(8,128)}, u32[]{:S(2)}) copy-start(f32[4,256,767]{2,1,0:T(8,128)} %copy-done.1) | copy-start | bytes 9424900
  856.0 187.6 %copy-start.42 = (f32[1024]{0:T(1024)S(1)}, f32[1024]{0:T(1024)}, u32[]{:S(2)}) copy-start(f32[1024]{0:T(1024)} %copy-done.41) | copy-start | bytes 12292
  856.0 187.6 %copy-start.46 = (f32[768]{0:T(1024)S(1)}, f32[768]{0:T(1024)}, u32[]{:S(2)}) copy-start(f32[768]{0:T(1024)} %param.15) | copy-start | bytes 9220
  (36 other events, 84.3 us)
Sparse Core Ops, SparseCore 0:
  33.1 21.6 all-gather.6
  56.4 19.7 all-gather.4
  88.2 121.0 all-reduce.5
  592.3 37.4 reduce-scatter.18
  730.6 37.4 reduce-scatter.20
  770.3 68.9 all-reduce.7
  842.5 34.0 reduce-scatter.24
  880.0 40.1 reduce-scatter.22
  922.6 121.0 all-reduce.9
  1047.4 41.4 reduce-scatter.16
  1092.8 42.3 reduce-scatter.14
Sparse Core Ops, SparseCore 1:
  90.5 23.8 all-gather.8
  116.1 23.8 all-gather.10
